TPU v7x, 32 devices: a whole 2x2x4 slice. The times are simulated.
32 devices in a mesh: illum: 2 (over x), box: 16 (over z, y, core).
Axes of the slice: x: 2, y: 2, z: 4, core: 2. Of those that a mesh axis runs over, the one named last changes fastest.
Arguments:
- patterns: bfloat16 [2, 256, 128, 256], P(None, 'box', None, 'illum'), parts along dimension 3, may hold values from -6 to 6
- owner_block: int32 [4], replicated, may hold values from 0 to 31
- low_index: int32 [256, 48], P('box'), may hold values from 0 to 315
- low_mask: int32 [256, 48], P('box'), may hold values 0 or 1
- low_table: bfloat16 [2, 316, 128], replicated, may hold values from -2 to 2
- interp: bfloat16 [128, 512], replicated, may hold values from -0.5 to 0.5
- shift_angle: float32 [8, 512], replicated, may hold values from -3.140625 to 3.140625
- par_source: int32 [32, 16], replicated, may hold values from 0 to 31, as said below
- par_index: int32 [32, 16], replicated, may hold values from 0 to 315
- par_mask: int32 [32, 16], replicated, may hold values 0 or 1
- par_table: bfloat16 [2, 316, 512], replicated, may hold values from -1.5 to 1.5
Outputs:
- incoming: float32 [2, 256, 128, 256], P(None, 'box', None, 'illum'), parts along dimension 3
There are 2 independent parts, one for each index of `illum`. A program takes and returns all parts, laid end to end along the dimension named above; an argument that names none is the same for every part. Nothing has to cross between parts.
Inputs may be any that keep to these rules, and one draw needn't show every extreme that they name: `par_source`: each parent's 16 slots name distinct parents other than itself.
All inputs are finite; a program needn't handle non-finite values. No bound on the sum of `low_mask` on one device may be relied on, other than what follows from the above.
Results may differ from a plain program's by a relative error of at most 0.0047.
Values may be sent and summed in bfloat16 or wider, within the bound.
A program may use at most 64 MiB of HBM per device.

v0:
```python
import functools

import jax
import jax.numpy as jnp
from jax import lax
from jax.experimental import pallas as pl
from jax.experimental.pallas import tpu as pltpu
from jax.sharding import PartitionSpec as P

F32 = jnp.float32
BF16 = jnp.bfloat16
MESH = pl.DeviceIdType.MESH


def dot(left, right):
    return jnp.dot(left, right, preferred_element_type=F32)


def kernel(
    n,
    listed,
    pitches,
    owner_ref,
    pat_ref,
    code_ref,
    table_ref,
    source_ref,
    index_ref,
    mask_ref,
    par_ref,
    interp_ref,
    angle_ref,
    out_ref,
    phase_ref,
    op,
    couple,
    parent,
    arrived,
    wide,
    result,
    result_send,
    returned,
    buf,
    landed,
    far,
    far_wide,
    own_wide,
    acc,
    out_send,
    out_recv,
    back_send,
    back_recv,
    rs_send,
    rs_recv,
    ag_send,
    ag_recv,
):
    me = lax.axis_index("box")
    boxes = pat_ref.shape[1]
    kdir, illums = pat_ref.shape[2], pat_ref.shape[3]
    groups8 = boxes // 8
    qdir = interp_ref.shape[1]
    qloc = qdir // n
    rows = 2 * listed * 8
    stages = n.bit_length() - 1
    kpitch, bpitch, qpitch, ppitch = pitches

    barrier = pltpu.get_barrier_semaphore()

    def greet(i, carry):
        peer = lax.rem(me + i, n)
        pl.semaphore_signal(barrier, inc=1, device_id={"box": peer}, device_id_type=MESH)
        return carry

    lax.fori_loop(1, n, greet, 0)

    for step in range(listed):
        owner = owner_ref[step]
        mine = owner // groups8 == me
        first = owner % groups8 * 8
        for part in range(2):
            block = pat_ref[part, pl.ds(first, 8)]
            buf[pl.ds((part * listed + step) * 8, 8)] = jnp.where(mine, block, jnp.zeros_like(block))

    pl.semaphore_wait(barrier, n - 1)

    half = rows // 2
    later = list(range(1, stages))
    cut = (stages + 1) // 2
    chains = [later, [b for b in later if b >= cut] + [b for b in later if b < cut]]

    def place(chain, depth):
        low = me % 2 * half + chain * (half // 2)
        size = half // 2
        for b in chains[chain][:depth]:
            size = size // 2
            low = low + me // (1 << b) % 2 * size
        return low, size

    def remote(src, dst, send, recv, bit):
        mine = me // (1 << bit) % 2
        return pltpu.make_async_remote_copy(
            src_ref=src,
            dst_ref=dst,
            send_sem=send,
            recv_sem=recv,
            device_id={"box": me + (1 - 2 * mine) * (1 << bit)},
            device_id_type=MESH,
        )

    def first_swap():
        give = (1 - me % 2) * half
        return remote(
            buf.at[pl.ds(give, half)], landed.at[pl.ds(0, half)], rs_send.at[0, 0], rs_recv.at[0, 0], 0
        )

    def halving(chain, depth):
        bit = chains[chain][depth]
        low, size = place(chain, depth)
        size = size // 2
        give = low + (1 - me // (1 << bit) % 2) * size
        spot = half + chain * (half // 2) + half // 2 - 2 * size
        return remote(
            buf.at[pl.ds(give, size)],
            landed.at[pl.ds(spot, size)],
            rs_send.at[chain, 1 + depth],
            rs_recv.at[chain, 1 + depth],
            bit,
        )

    def halve(chain, depth):
        halving(chain, depth).wait()
        low, size = place(chain, depth + 1)
        spot = half + chain * (half // 2) + half // 2 - 2 * size
        target = far if depth + 1 == len(later) else buf
        target[pl.ds(low, size)] = buf[pl.ds(low, size)] + landed[pl.ds(spot, size)]
        if depth + 1 < len(later):
            halving(chain, depth + 1).start()
        else:
            doubling(chain, len(later)).start()

    def doubling(chain, depth):
        low, size = place(chain, depth)
        bit = chains[chain][depth - 1] if depth else 0
        spots = far.at[pl.ds(low, size)]
        return remote(spots, spots, ag_send.at[chain, depth], ag_recv.at[chain, depth], bit)

    def double(chain, depth):
        doubling(chain, depth).wait()
        doubling(chain, depth - 1).start()

    first_swap().start()
    phase_ref[:, :8] = jnp.cos(angle_ref[...]).T
    phase_ref[:, 8:] = jnp.sin(angle_ref[...]).T

    tile = 256
    for parent_at in range(groups8):

        def lift(t, carry, parent_at=parent_at):
            at = pl.multiple_of(t * tile, tile)
            left = interp_ref[:, pl.ds(at, tile)].T
            real = jnp.zeros((tile, illums), F32)
            imag = jnp.zeros((tile, illums), F32)
            for child in range(8):
                b = parent_at * 8 + child
                both = dot(left, jnp.concatenate([pat_ref[0, b], pat_ref[1, b]], axis=1))
                cosine = phase_ref[pl.ds(at, tile), child : child + 1]
                sine = phase_ref[pl.ds(at, tile), 8 + child : 9 + child]
                re, im = both[:, :illums], both[:, illums:]
                real = real + (cosine * re - sine * im)
                imag = imag + (cosine * im + sine * re)
            parent[parent_at, pl.ds(at, tile), :] = real.astype(BF16)
            parent[groups8 + parent_at, pl.ds(at, tile), :] = imag.astype(BF16)
            return carry

        lax.fori_loop(0, qdir // tile, lift, 0)

    def out_copy(i):
        peer = lax.rem(me + i, n)
        return pltpu.make_async_remote_copy(
            src_ref=parent.at[:, pl.ds(pl.multiple_of(peer * qloc, qloc), qloc), :],
            dst_ref=arrived.at[me],
            send_sem=out_send.at[i],
            recv_sem=out_recv.at[i],
            device_id={"box": peer},
            device_id_type=MESH,
        )

    def start_out(i, carry):
        out_copy(i).start()
        return carry

    lax.fori_loop(1, n, start_out, 0)

    first_swap().wait()
    kept = pl.ds(me % 2 * half, half)
    buf[kept] = buf[kept] + landed[pl.ds(0, half)]
    halving(0, 0).start()
    halving(1, 0).start()

    unroll = 8
    parents = n * groups8
    parents2 = 2 * parents

    lanes = lax.broadcasted_iota(jnp.int32, (parents, parents), 1)
    code = jnp.zeros((parents, parents), jnp.int32)
    slot_code = jnp.where(mask_ref[...] > 0, index_ref[...] + 1, 0).T
    slot_source = source_ref[...].T
    for j in range(source_ref.shape[0]):
        code = code + jnp.where(slot_source[:, j : j + 1] == lanes, slot_code[:, j : j + 1], 0)
    code = jnp.concatenate([code, code], axis=1) - 1
    each = max(1, 256 // parents2)
    kinds = lax.broadcasted_iota(jnp.int32, (par_ref.shape[1], each * parents2), 0)
    first = lax.broadcasted_iota(jnp.int32, (qloc, parents2), 1) < parents
    for p in range(0, parents, each):
        row = jnp.concatenate([code[p + u : p + u + 1] for u in range(each)], axis=1)
        hot = jnp.where(kinds == row, 1.0, 0.0).astype(BF16)
        got = dot(par_ref[...], hot)
        for u in range(each):
            real = got[:qloc, u * parents2 : (u + 1) * parents2]
            imag = got[qloc:, u * parents2 : (u + 1) * parents2]
            couple[pl.ds(p + u, qloc, stride=ppitch), :] = jnp.where(first, real, -imag)
            couple[pl.ds(parents + p + u, qloc, stride=ppitch), :] = jnp.where(first, imag, real)

    width = code_ref.shape[1]
    low_kinds = lax.broadcasted_iota(jnp.int32, (table_ref.shape[1], 2 * width), 0)
    lane = lax.broadcasted_iota(jnp.int32, (kdir, width), 1)
    flip = me % 2
    column = jnp.where(
        lane < 2 * boxes, lane // boxes, jnp.where(lane < 2 * boxes + half, flip, 1 - flip)
    )
    low_first = column == 0
    for b in range(0, boxes, 2):
        row = jnp.concatenate([code_ref[b : b + 1], code_ref[b + 1 : b + 2]], axis=1)
        hot = jnp.where(low_kinds == row, 1.0, 0.0).astype(BF16)
        got = dot(table_ref[...], hot)
        for u in range(2):
            real = got[:kdir, u * width : (u + 1) * width]
            imag = got[kdir:, u * width : (u + 1) * width]
            op[pl.ds(b + u, kdir, stride=bpitch), :] = jnp.where(low_first, real, -imag)
            op[pl.ds(boxes + b + u, kdir, stride=bpitch), :] = jnp.where(low_first, imag, real)

    def operator(k):
        return op[pl.ds(pl.multiple_of(k * bpitch, 8), 2 * boxes), :].astype(BF16)

    for chain in range(2):
        halve(chain, 0)

    def widen(source, value):
        for part in range(2):
            for p in range(groups8):
                s = (part * n + source) * groups8 + p
                at = pl.multiple_of(s * qpitch, 8)
                wide[pl.ds(at, qloc), :] = value(part * groups8 + p).astype(F32)

    widen(me, lambda c: parent[c, pl.ds(pl.multiple_of(me * qloc, qloc), qloc), :])

    def take(i, carry):
        out_copy(i).wait()
        source = lax.rem(me - i + n, n)
        widen(source, lambda c: arrived[source, c])
        return carry

    lax.fori_loop(1, n, take, 0)
    def translate(t, carry):
        for u in range(unroll):
            q = t * unroll + u
            sources = wide[pl.ds(q, parents2, stride=qpitch), :].astype(BF16)
            result[pl.ds(q, parents2, stride=qpitch), :] = dot(
                couple[pl.ds(pl.multiple_of(q * ppitch, 8), parents2), :].astype(BF16), sources
            )
        return carry

    lax.fori_loop(0, qloc // unroll, translate, 0)
    for s in range(parents2):
        result_send[s // parents, s % parents] = result[pl.ds(s * qpitch, qloc), :].astype(BF16)

    def back_copy(i):
        peer = lax.rem(me + i, n)
        return pltpu.make_async_remote_copy(
            src_ref=result_send.at[:, pl.ds(peer * groups8, groups8)],
            dst_ref=returned.at[:, :, pl.ds(pl.multiple_of(me * qloc, qloc), qloc), :],
            send_sem=back_send.at[i],
            recv_sem=back_recv.at[i],
            device_id={"box": peer},
            device_id_type=MESH,
        )

    def start_back(i, carry):
        back_copy(i).start()
        return carry

    lax.fori_loop(1, n, start_back, 0)
    returned[:, :, pl.ds(pl.multiple_of(me * qloc, qloc), qloc), :] = result_send[:, pl.ds(me * groups8, groups8)]

    for chain in range(2):
        halve(chain, 1)

    for part in range(2):
        for b in range(boxes):
            own_wide[pl.ds((part * boxes + b) * kpitch, kdir), :] = pat_ref[part, b].astype(F32)

    def near_own(t, carry):
        sums = []
        for u in range(unroll):
            k = t * unroll + u
            sources = own_wide[pl.ds(k, 2 * boxes, stride=kpitch), :].astype(BF16)
            sums.append(dot(operator(k)[:, : 2 * boxes], sources))
        for u in range(unroll):
            acc[pl.ds(t * unroll + u, 2 * boxes, stride=kpitch), :] = sums[u]
        return carry

    lax.fori_loop(0, kdir // unroll, near_own, 0)

    for depth in range(2, len(later)):
        for chain in range(2):
            halve(chain, depth)
    for depth in range(len(later), 1, -1):
        for chain in range(2):
            double(chain, depth)

    def land(i, carry):
        back_copy(i).wait()
        return carry

    lax.fori_loop(1, n, land, 0)

    for parent_at in range(groups8):
        for child in range(8):
            b = parent_at * 8 + child
            re = returned[0, parent_at].astype(F32)
            im = returned[1, parent_at].astype(F32)
            cosine = phase_ref[:, child : child + 1]
            sine = phase_ref[:, 8 + child : 9 + child]
            real = (cosine * re + sine * im).astype(BF16)
            imag = (cosine * im - sine * re).astype(BF16)
            both = dot(interp_ref[...], jnp.concatenate([real, imag], axis=1))
            spots = pl.ds(b * kdir, kdir)
            out_ref[spots, :] = both[:, :illums]
            spots = pl.ds((boxes + b) * kdir, kdir)
            out_ref[spots, :] = both[:, illums:]

    for chain in range(2):
        double(chain, 1)

    def near_half(part, at):
        def widen_far(j, carry):
            far_wide[pl.ds(pl.multiple_of(j * kpitch, 8), kdir), :] = far[part * half + j].astype(F32)
            return carry

        lax.fori_loop(0, half, widen_far, 0)

        def near_far(t, carry):
            sums = []
            for u in range(unroll):
                k = t * unroll + u
                sources = far_wide[pl.ds(k, half, stride=kpitch), :].astype(BF16)
                spots = pl.ds(k, 2 * boxes, stride=kpitch)
                sums.append(acc[spots, :] + dot(operator(k)[:, at : at + half], sources))
            for u in range(unroll):
                acc[pl.ds(t * unroll + u, 2 * boxes, stride=kpitch), :] = sums[u]
            return carry

        lax.fori_loop(0, kdir // unroll, near_far, 0)

    near_half(me % 2, 2 * boxes)
    for chain in range(2):
        doubling(chain, 0).wait()
    near_half(1 - me % 2, 2 * boxes + half)

    for b in range(2 * boxes):
        spots = pl.ds(b * kdir, kdir)
        out_ref[spots, :] = out_ref[spots, :] + acc[pl.ds(b * kpitch, kdir), :]


def shards(
    patterns,
    owner_block,
    low_index,
    low_mask,
    low_table,
    interp,
    shift_angle,
    par_source,
    par_index,
    par_mask,
    par_table,
):
    boxes, kdir, illums = patterns.shape[1:]
    groups8 = boxes // 8
    qdir = interp.shape[1]
    n = lax.axis_size("box")
    listed = owner_block.shape[0]
    parents = par_source.shape[0]
    qloc = qdir // n
    rows = 2 * listed * 8
    sources = low_index.shape[1]

    code = jnp.where(low_mask > 0, low_index, -1)
    own, listed_code = code[:, :boxes], code[:, boxes:]
    spare = jnp.full((boxes, -2 * sources % 128), -1, jnp.int32)
    code = jnp.concatenate([own, own, listed_code, listed_code, spare], axis=1)
    low = jnp.transpose(low_table, (0, 2, 1)).reshape(2 * kdir, -1)
    start = lax.axis_index("box") * qloc
    table = lax.dynamic_slice_in_dim(par_table, start, qloc, 2)
    table = jnp.transpose(table, (0, 2, 1)).reshape(2 * qloc, -1)

    pitches = (kdir + 8, 2 * boxes + 8, qloc + 8, 2 * parents + 8)
    kpitch, bpitch, qpitch, ppitch = pitches
    vmem = pl.BlockSpec(memory_space=pltpu.VMEM)
    smem = pl.BlockSpec(memory_space=pltpu.SMEM)
    stages = n.bit_length() - 1
    dma = pltpu.SemaphoreType.DMA
    return pl.pallas_call(
        functools.partial(kernel, n, listed, pitches),
        out_shape=jax.ShapeDtypeStruct((2 * boxes * kdir, illums), F32),
        in_specs=[smem] + [vmem] * 9,
        out_specs=vmem,
        scratch_shapes=[
            pltpu.VMEM((qdir, 16), F32),
            pltpu.VMEM((kdir * bpitch, code.shape[1]), F32),
            pltpu.VMEM((qloc * ppitch, 2 * parents), F32),
            pltpu.VMEM((2 * groups8, qdir, illums), BF16),
            pltpu.VMEM((n, 2 * groups8, qloc, illums), BF16),
            pltpu.VMEM((2 * parents * qpitch, illums), F32),
            pltpu.VMEM((2 * parents * qpitch, illums), F32),
            pltpu.VMEM((2, parents, qloc, illums), BF16),
            pltpu.VMEM((2, groups8, qdir, illums), BF16),
            pltpu.VMEM((rows, kdir, illums), BF16),
            pltpu.VMEM((rows, kdir, illums), BF16),
            pltpu.VMEM((rows, kdir, illums), BF16),
            pltpu.VMEM((rows // 2 * kpitch, illums), F32),
            pltpu.VMEM((2 * boxes * kpitch, illums), F32),
            pltpu.VMEM((2 * boxes * kpitch, illums), F32),
            dma((n,)),
            dma((n,)),
            dma((n,)),
            dma((n,)),
            dma((2, stages)),
            dma((2, stages)),
            dma((2, stages)),
            dma((2, stages)),
        ],
        compiler_params=pltpu.CompilerParams(
            collective_id=0, has_side_effects=True, vmem_limit_bytes=56 * 1024 * 1024
        ),
    )(
        owner_block,
        patterns,
        code,
        low,
        par_source.T,
        par_index.T,
        par_mask.T,
        table,
        interp,
        shift_angle,
    ).reshape(2, boxes, kdir, illums)


def solution(mesh):
    placed = (
        P(None, "box", None, "illum"),
        P(),
        P("box", None),
        P("box", None),
        P(),
        P(),
        P(),
        P(),
        P(),
        P(),
        P(),
    )
    return jax.shard_map(
        shards, mesh=mesh, in_specs=placed, out_specs=P(None, "box", None, "illum"), check_vma=False
    )
```

profile of v0, /device:TPU:0, one launch (start us, length us, event | category | flops | bytes accessed | tf_op | source)
XLA Modules:
  0.0 82.4 jit_solution(3620261191129111772)
XLA Ops:
  0.0 0.0 copy-start
  0.0 0.1 pad.3.clone
  0.1 0.8 compare_select_fusion
  0.8 0.1 slice.10
  0.9 0.7 add_add_fusion.code_ref
  1.6 0.0 copy-done
  1.6 0.2 dynamic-slice_bitcast_fusion
  1.8 0.8 copy.13
  2.6 1.7 %copy.12 = bf16[2,128,316]{2,1,0:T(8,128)(2,1)} copy(bf16[2,128,316]{1,0,2:T(2,128)(2,1)} %bitcast.13) | data formatting | bytes 323584 | tf_op jit(solution)/shard_map/transpose | solution.py:403
  4.3 74.9 %shard_map.109 = f32[4096,128]{1,0:T(8,128)} custom-call(s32[4]{0:T(128)} %owner_ref.1, bf16[2,16,128,128]{3,2,1,0:T(8,128)(2,1)} %pat_ref.1, s32[16,128]{1,0:T(8,128)} %add_add_fusion.code_ref, bf16[256,316]{1,0:T(8,128)(2,1)} %bitcast.11, s32[16,32]{1,0:T(8,128)} %bitcast.15, s32[16,32]{1,0:T(8,128)} %bitcast.16, s32[16,32]{1,0:T(8,128)} %bitcast.17, ...), custom_call_target="tpu_custom_call" | custom-call | tf_op jit(solution)/shard_map/pallas_call | solution.py:414
  79.2 3.1 %copy.15 = f32[2,16,128,128]{3,2,1,0:T(8,128)} copy(f32[2,16,128,128]{3,2,1,0:T(8,128)} %bitcast.10) | data formatting | bytes 4194304
  (1 shorter events, 0.0 us)
Async XLA Ops:
  0.0 1.6 %copy-start = (bf16[2,316,512]{2,0,1:T(2,128)(2,1)S(1)}, bf16[2,316,512]{2,0,1:T(2,128)(2,1)}, u32[]{:S(2)}) copy-start(bf16[2,316,512]{2,0,1:T(2,128)(2,1)} %param.21) | copy-start | bytes 1941508
where the time goes:
time: 82.7 us; the launch traced here: 82.4 us
  Pallas kernels  74.9 us (91%)
  local copies, waits for them, and re-layouts  6.03 us (7%)
  other arithmetic  1.44 us (2%)
    pallas_call x1, Pallas kernels, shards(): pl.pallas_call(functools.partial(kernel, n, listed, pitches), out_shape=j...  74.9 us
    unnamed x3, local copies, waits for them, and re-layouts  3.14 us
    transpose x1, local copies, waits for them, and re-layouts, shards(): low = jnp.transpose(low_table, (0, 2, 1)).reshape(2 * kdir, -1)  1.74 us

commit v1 on v0

v1 whole, which is shorter than its diff:
```python
import functools

import jax
import jax.numpy as jnp
from jax import lax
from jax.experimental import pallas as pl
from jax.experimental.pallas import tpu as pltpu
from jax.sharding import PartitionSpec as P

F32 = jnp.float32
BF16 = jnp.bfloat16
MESH = pl.DeviceIdType.MESH


def dot(left, right):
    return jnp.dot(left, right, preferred_element_type=F32)


def kernel(
    n,
    listed,
    chains,
    pitches,
    owner_ref,
    pat_ref,
    code_ref,
    table_ref,
    source_ref,
    index_ref,
    mask_ref,
    par_ref,
    interp_ref,
    angle_ref,
    out_ref,
    phase_ref,
    op,
    couple,
    parent,
    arrived,
    wide,
    result,
    result_send,
    returned,
    own,
    given,
    buf,
    landed,
    far,
    own_wide,
    acc,
    out_send,
    out_recv,
    back_send,
    back_recv,
    swap_send,
    swap_recv,
    rs_send,
    rs_recv,
    ag_send,
    ag_recv,
):
    me = lax.axis_index("box")
    core = me % 2
    boxes = pat_ref.shape[1]
    kdir, illums = pat_ref.shape[2], pat_ref.shape[3]
    groups8 = boxes // 8
    qdir = interp_ref.shape[1]
    qloc = qdir // n
    both_own = 2 * boxes
    span = kdir // 2 // chains
    order = list(range(1, n.bit_length() - 1))
    kpitch, bpitch, qpitch, ppitch = pitches

    barrier = pltpu.get_barrier_semaphore()

    def greet(i, carry):
        peer = lax.rem(me + i, n)
        pl.semaphore_signal(barrier, inc=1, device_id={"box": peer}, device_id_type=MESH)
        return carry

    lax.fori_loop(1, n, greet, 0)

    unroll = 8
    for part in range(2):
        for b in range(boxes):
            spot = b // 8 * 16 + part * 8 + b % 8
            own_wide[pl.ds(spot * kpitch, kdir), :] = pat_ref[part, b].astype(F32)

    def turn(t, carry):
        for u in range(unroll):
            k = t * unroll + u
            own[k] = own_wide[pl.ds(k, both_own, stride=kpitch), :].astype(BF16)
        return carry

    lax.fori_loop(0, kdir // unroll, turn, 0)

    def remote(src, dst, send, recv, bit):
        mine = me // (1 << bit) % 2
        return pltpu.make_async_remote_copy(
            src_ref=src,
            dst_ref=dst,
            send_sem=send,
            recv_sem=recv,
            device_id={"box": me + (1 - 2 * mine) * (1 << bit)},
            device_id_type=MESH,
        )

    def swap(chain):
        spots = own.at[pl.ds((1 - core) * (kdir // 2) + chain * span, span)]
        return remote(spots, given[chain], swap_send.at[chain], swap_recv.at[chain], 0)

    def place(chain, depth):
        low = core * (kdir // 2) + chain * span
        size = span
        for b in order[:depth]:
            size = size // 2
            low = low + me // (1 << b) % 2 * size
        return low, size

    def halving(chain, depth):
        bit = order[depth]
        low, size = place(chain, depth)
        size = size // 2
        give = low + (1 - me // (1 << bit) % 2) * size
        spot = chain * span + span - 2 * size
        return remote(
            buf.at[pl.ds(give, size)],
            landed.at[pl.ds(spot, size)],
            rs_send.at[chain, depth],
            rs_recv.at[chain, depth],
            bit,
        )

    def halve(chain, depth):
        halving(chain, depth).wait()
        low, size = place(chain, depth + 1)
        spot = chain * span + span - 2 * size
        target = far if depth + 1 == len(order) else buf
        target[pl.ds(low, size)] = buf[pl.ds(low, size)] + landed[pl.ds(spot, size)]
        if depth + 1 < len(order):
            halving(chain, depth + 1).start()
        else:
            doubling(chain, len(order)).start()

    def doubling(chain, depth):
        low, size = place(chain, depth)
        bit = order[depth - 1] if depth else 0
        spots = far.at[pl.ds(low, size)]
        return remote(spots, spots, ag_send.at[chain, depth], ag_recv.at[chain, depth], bit)

    def double(chain, depth):
        doubling(chain, depth).wait()
        doubling(chain, depth - 1).start()

    def merge(chain):
        swap(chain).wait()
        low, size = place(chain, 0)
        for step in range(listed):
            owner = owner_ref[step]
            device = owner // groups8
            rows = pl.ds(owner % groups8 * 16, 16)
            block = own[pl.ds(low, size), rows, :]
            theirs = given[chain][:, rows, :]
            block = jnp.where(device == me, block, jnp.where(device // 2 == me // 2, theirs, jnp.zeros_like(block)))
            buf[pl.ds(low, size), step * 16 : step * 16 + 16, :] = block
        halving(chain, 0).start()

    pl.semaphore_wait(barrier, n - 1)
    for chain in range(chains):
        swap(chain).start()
    phase_ref[:, :8] = jnp.cos(angle_ref[...]).T
    phase_ref[:, 8:] = jnp.sin(angle_ref[...]).T
    for chain in range(chains):
        merge(chain)

    def out_copy(i, parent_at):
        peer = lax.rem(me + i, n)
        return pltpu.make_async_remote_copy(
            src_ref=parent.at[pl.ds(2 * parent_at, 2), pl.ds(pl.multiple_of(peer * qloc, qloc), qloc), :],
            dst_ref=arrived.at[me, pl.ds(2 * parent_at, 2)],
            send_sem=out_send.at[parent_at, i],
            recv_sem=out_recv.at[parent_at, i],
            device_id={"box": peer},
            device_id_type=MESH,
        )

    tile = 256
    for parent_at in range(groups8):

        def lift(t, carry, parent_at=parent_at):
            at = pl.multiple_of(t * tile, tile)
            left = interp_ref[:, pl.ds(at, tile)].T
            real = jnp.zeros((tile, illums), F32)
            imag = jnp.zeros((tile, illums), F32)
            for child in range(8):
                b = parent_at * 8 + child
                both = dot(left, jnp.concatenate([pat_ref[0, b], pat_ref[1, b]], axis=1))
                cosine = phase_ref[pl.ds(at, tile), child : child + 1]
                sine = phase_ref[pl.ds(at, tile), 8 + child : 9 + child]
                re, im = both[:, :illums], both[:, illums:]
                real = real + (cosine * re - sine * im)
                imag = imag + (cosine * im + sine * re)
            parent[2 * parent_at, pl.ds(at, tile), :] = real.astype(BF16)
            parent[2 * parent_at + 1, pl.ds(at, tile), :] = imag.astype(BF16)
            return carry

        lax.fori_loop(0, qdir // tile, lift, 0)

        def start_out(i, carry, parent_at=parent_at):
            out_copy(i, parent_at).start()
            return carry

        lax.fori_loop(1, n, start_out, 0)

    parents = n * groups8
    parents2 = 2 * parents

    lanes = lax.broadcasted_iota(jnp.int32, (parents, parents), 1)
    code = jnp.zeros((parents, parents), jnp.int32)
    slot_code = jnp.where(mask_ref[...] > 0, index_ref[...] + 1, 0).T
    slot_source = source_ref[...].T
    for j in range(source_ref.shape[0]):
        code = code + jnp.where(slot_source[:, j : j + 1] == lanes, slot_code[:, j : j + 1], 0)
    code = jnp.concatenate([code, code], axis=1) - 1
    each = max(1, 256 // parents2)
    kinds = lax.broadcasted_iota(jnp.int32, (par_ref.shape[1], each * parents2), 0)
    first = lax.broadcasted_iota(jnp.int32, (qloc, parents2), 1) < parents
    for p in range(0, parents, each):
        row = jnp.concatenate([code[p + u : p + u + 1] for u in range(each)], axis=1)
        hot = jnp.where(kinds == row, 1.0, 0.0).astype(BF16)
        got = dot(par_ref[...], hot)
        for u in range(each):
            real = got[:qloc, u * parents2 : (u + 1) * parents2]
            imag = got[qloc:, u * parents2 : (u + 1) * parents2]
            couple[pl.ds(p + u, qloc, stride=ppitch), :] = jnp.where(first, real, -imag)
            couple[pl.ds(parents + p + u, qloc, stride=ppitch), :] = jnp.where(first, imag, real)

    for chain in range(chains):
        halve(chain, 0)

    width = code_ref.shape[1]
    low_kinds = lax.broadcasted_iota(jnp.int32, (table_ref.shape[1], 2 * width), 0)
    low_first = lax.broadcasted_iota(jnp.int32, (kdir, width), 1) // 8 % 2 == 0
    for b in range(0, boxes, 2):
        row = jnp.concatenate([code_ref[b : b + 1], code_ref[b + 1 : b + 2]], axis=1)
        hot = jnp.where(low_kinds == row, 1.0, 0.0).astype(BF16)
        got = dot(table_ref[...], hot)
        for u in range(2):
            real = got[:kdir, u * width : (u + 1) * width]
            imag = got[kdir:, u * width : (u + 1) * width]
            op[pl.ds(b + u, kdir, stride=bpitch), :] = jnp.where(low_first, real, -imag)
            op[pl.ds(boxes + b + u, kdir, stride=bpitch), :] = jnp.where(low_first, imag, real)

    for depth in range(1, len(order)):
        for chain in range(chains):
            halve(chain, depth)
    for depth in range(len(order), 1, -1):
        for chain in range(chains):
            double(chain, depth)

    def widen(source, value):
        for part in range(2):
            for p in range(groups8):
                s = (part * n + source) * groups8 + p
                at = pl.multiple_of(s * qpitch, 8)
                wide[pl.ds(at, qloc), :] = value(p * 2 + part).astype(F32)

    widen(me, lambda c: parent[c, pl.ds(pl.multiple_of(me * qloc, qloc), qloc), :])

    def take(i, carry):
        for parent_at in range(groups8):
            out_copy(i, parent_at).wait()
        source = lax.rem(me - i + n, n)
        widen(source, lambda c: arrived[source, c])
        return carry

    lax.fori_loop(1, n, take, 0)

    def translate(t, carry):
        for u in range(unroll):
            q = t * unroll + u
            sources = wide[pl.ds(q, parents2, stride=qpitch), :].astype(BF16)
            result[pl.ds(q, parents2, stride=qpitch), :] = dot(
                couple[pl.ds(pl.multiple_of(q * ppitch, 8), parents2), :].astype(BF16), sources
            )
        return carry

    lax.fori_loop(0, qloc // unroll, translate, 0)
    for s in range(parents2):
        result_send[s // parents, s % parents] = result[pl.ds(s * qpitch, qloc), :].astype(BF16)

    def back_copy(i):
        peer = lax.rem(me + i, n)
        return pltpu.make_async_remote_copy(
            src_ref=result_send.at[:, pl.ds(peer * groups8, groups8)],
            dst_ref=returned.at[:, :, pl.ds(pl.multiple_of(me * qloc, qloc), qloc), :],
            send_sem=back_send.at[i],
            recv_sem=back_recv.at[i],
            device_id={"box": peer},
            device_id_type=MESH,
        )

    def start_back(i, carry):
        back_copy(i).start()
        return carry

    lax.fori_loop(1, n, start_back, 0)
    returned[:, :, pl.ds(pl.multiple_of(me * qloc, qloc), qloc), :] = result_send[:, pl.ds(me * groups8, groups8)]

    def near(at):
        def one(t, carry):
            sums = []
            for u in range(unroll):
                k = at + t * unroll + u
                operator = op[pl.ds(pl.multiple_of(k * bpitch, 8), both_own), :].astype(BF16)
                sources = jnp.concatenate([own[k], far[k]], axis=0)
                sums.append(dot(operator[:, : both_own + 16 * listed], sources))
            for u in range(unroll):
                acc[pl.ds(at + t * unroll + u, both_own, stride=kpitch), :] = sums[u]
            return carry

        lax.fori_loop(0, span // unroll, one, 0)

    for chain in range(chains):
        double(chain, 1)
        near(core * (kdir // 2) + chain * span)

    for chain in range(chains):
        doubling(chain, 0).wait()
        near((1 - core) * (kdir // 2) + chain * span)

    def land(i, carry):
        back_copy(i).wait()
        return carry

    lax.fori_loop(1, n, land, 0)

    for parent_at in range(groups8):
        for child in range(8):
            b = parent_at * 8 + child
            re = returned[0, parent_at].astype(F32)
            im = returned[1, parent_at].astype(F32)
            cosine = phase_ref[:, child : child + 1]
            sine = phase_ref[:, 8 + child : 9 + child]
            real = (cosine * re + sine * im).astype(BF16)
            imag = (cosine * im - sine * re).astype(BF16)
            both = dot(interp_ref[...], jnp.concatenate([real, imag], axis=1))
            out_ref[pl.ds(b * kdir, kdir), :] = both[:, :illums] + acc[pl.ds(b * kpitch, kdir), :]
            out_ref[pl.ds((boxes + b) * kdir, kdir), :] = (
                both[:, illums:] + acc[pl.ds((boxes + b) * kpitch, kdir), :]
            )


def shards(
    patterns,
    owner_block,
    low_index,
    low_mask,
    low_table,
    interp,
    shift_angle,
    par_source,
    par_index,
    par_mask,
    par_table,
):
    boxes, kdir, illums = patterns.shape[1:]
    groups8 = boxes // 8
    qdir = interp.shape[1]
    n = lax.axis_size("box")
    listed = owner_block.shape[0]
    parents = par_source.shape[0]
    qloc = qdir // n
    sources = low_index.shape[1]
    chains = 4

    code = jnp.where(low_mask > 0, low_index, -1)
    code = jnp.repeat(code.reshape(boxes, sources // 8, 1, 8), 2, axis=2).reshape(boxes, 2 * sources)
    code = jnp.pad(code, ((0, 0), (0, -2 * sources % 128)), constant_values=-1)
    low = jnp.transpose(low_table, (0, 2, 1)).reshape(2 * kdir, -1)
    start = lax.axis_index("box") * qloc
    table = lax.dynamic_slice_in_dim(par_table, start, qloc, 2)
    table = jnp.transpose(table, (0, 2, 1)).reshape(2 * qloc, -1)

    pitches = (kdir + 8, 2 * boxes + 8, qloc + 8, 2 * parents + 8)
    kpitch, bpitch, qpitch, ppitch = pitches
    vmem = pl.BlockSpec(memory_space=pltpu.VMEM)
    smem = pl.BlockSpec(memory_space=pltpu.SMEM)
    stages = n.bit_length() - 1
    dma = pltpu.SemaphoreType.DMA
    return pl.pallas_call(
        functools.partial(kernel, n, listed, chains, pitches),
        out_shape=jax.ShapeDtypeStruct((2 * boxes * kdir, illums), F32),
        in_specs=[smem] + [vmem] * 9,
        out_specs=vmem,
        scratch_shapes=[
            pltpu.VMEM((qdir, 16), F32),
            pltpu.VMEM((kdir * bpitch, code.shape[1]), F32),
            pltpu.VMEM((qloc * ppitch, 2 * parents), F32),
            pltpu.VMEM((2 * groups8, qdir, illums), BF16),
            pltpu.VMEM((n, 2 * groups8, qloc, illums), BF16),
            pltpu.VMEM((2 * parents * qpitch, illums), F32),
            pltpu.VMEM((2 * parents * qpitch, illums), F32),
            pltpu.VMEM((2, parents, qloc, illums), BF16),
            pltpu.VMEM((2, groups8, qdir, illums), BF16),
            pltpu.VMEM((kdir, 2 * boxes, illums), BF16),
            [pltpu.VMEM((kdir // 2 // chains, 2 * boxes, illums), BF16) for _ in range(chains)],
            pltpu.VMEM((kdir, 16 * listed, illums), BF16),
            pltpu.VMEM((kdir // 2, 16 * listed, illums), BF16),
            pltpu.VMEM((kdir, 16 * listed, illums), BF16),
            pltpu.VMEM((2 * boxes * kpitch, illums), F32),
            pltpu.VMEM((2 * boxes * kpitch, illums), F32),
            dma((groups8, n)),
            dma((groups8, n)),
            dma((n,)),
            dma((n,)),
            dma((chains,)),
            dma((chains,)),
            dma((chains, stages)),
            dma((chains, stages)),
            dma((chains, stages)),
            dma((chains, stages)),
        ],
        compiler_params=pltpu.CompilerParams(
            collective_id=0, has_side_effects=True, vmem_limit_bytes=56 * 1024 * 1024
        ),
    )(
        owner_block,
        patterns,
        code,
        low,
        par_source.T,
        par_index.T,
        par_mask.T,
        table,
        interp,
        shift_angle,
    ).reshape(2, boxes, kdir, illums)


def solution(mesh):
    placed = (
        P(None, "box", None, "illum"),
        P(),
        P("box", None),
        P("box", None),
        P(),
        P(),
        P(),
        P(),
        P(),
        P(),
        P(),
    )
    return jax.shard_map(
        shards, mesh=mesh, in_specs=placed, out_specs=P(None, "box", None, "illum"), check_vma=False
    )
```

time: 82.7 us -> 73.2 us (0.89)
  Pallas kernels: 74.9 us -> 64.7 us
  local copies, waits for them, and re-layouts: 6.03 us -> 8.17 us
  other arithmetic: 1.44 us -> 0.01 us
    pallas_call x1, Pallas kernels: 74.9 us -> 64.7 us  [shards(): pl.pallas_call(functools.partial(kernel, n, listed, chains, pitches), out...]
    unnamed x3 -> x5, local copies, waits for them, and re-layouts: 3.14 us -> 4.76 us
where the time goes in v1:
time: 73.2 us; the launch traced here: 72.9 us
  Pallas kernels  64.7 us (88%)
  local copies, waits for them, and re-layouts  8.17 us (11%)
    pallas_call x1, Pallas kernels, shards(): pl.pallas_call(functools.partial(kernel, n, listed, chains, pitches), out...  64.7 us
    unnamed x5, local copies, waits for them, and re-layouts  4.76 us
    transpose x1, local copies, waits for them, and re-layouts, shards(): low = jnp.transpose(low_table, (0, 2, 1)).reshape(2 * kdir, -1)  1.74 us

profile of v1, /device:TPU:0, one launch (start us, length us, event | category | flops | bytes accessed | tf_op | source)
XLA Modules:
  0.0 72.9 jit_solution(3805330856009166232)
XLA Ops:
  0.0 0.0 copy-start
  0.0 0.8 %copy.15 = s32[16,48]{0,1:T(8,128)S(1)} copy(s32[16,48]{1,0:T(8,128)} %param.13) | data formatting | bytes 6144 | tf_op args[2]
  0.8 0.8 %copy.14 = s32[16,48]{0,1:T(8,128)S(1)} copy(s32[16,48]{1,0:T(8,128)} %param.14) | data formatting | bytes 6144 | tf_op args[3]
  1.6 0.1 copy.16
  1.7 0.6 pad.4.code_ref
  2.3 0.0 copy-done
  2.3 0.2 dynamic-slice_bitcast_fusion
  2.6 0.8 %copy.18 = bf16[2,32,316]{2,1,0:T(8,128)(2,1)} copy(bf16[2,32,316]{1,0,2:T(2,128)(2,1)S(1)} %dynamic-slice_bitcast_fusion) | data formatting | bytes 80896 | tf_op jit(solution)/shard_map/transpose | solution.py:383
  3.3 1.7 %copy.17 = bf16[2,128,316]{2,1,0:T(8,128)(2,1)} copy(bf16[2,128,316]{1,0,2:T(2,128)(2,1)} %bitcast.16) | data formatting | bytes 323584 | tf_op jit(solution)/shard_map/transpose | solution.py:380
  5.1 64.7 %shard_map.109 = f32[4096,128]{1,0:T(8,128)} custom-call(s32[4]{0:T(128)} %owner_ref.1, bf16[2,16,128,128]{3,2,1,0:T(8,128)(2,1)} %pat_ref.1, s32[16,128]{1,0:T(8,128)} %pad.4.code_ref, bf16[256,316]{1,0:T(8,128)(2,1)} %bitcast.13, s32[16,32]{1,0:T(8,128)} %bitcast.17, s32[16,32]{1,0:T(8,128)} %bitcast.18, s32[16,32]{1,0:T(8,128)} %bitcast.19, ...), custom_call_target="tpu_custom_call" | custom-call | tf_op jit(solution)/shard_map/pallas_call | solution.py:391
  69.8 3.1 %copy.20 = f32[2,16,128,128]{3,2,1,0:T(8,128)} copy(f32[2,16,128,128]{3,2,1,0:T(8,128)} %bitcast.12) | data formatting | bytes 4194304
  (2 shorter events, 0.0 us)
Async XLA Ops:
  0.0 2.3 %copy-start = (bf16[2,316,512]{2,0,1:T(2,128)(2,1)S(1)}, bf16[2,316,512]{2,0,1:T(2,128)(2,1)}, u32[]{:S(2)}) copy-start(bf16[2,316,512]{2,0,1:T(2,128)(2,1)} %param.21) | copy-start | bytes 1941508

commit v2 on v1

v2 whole, which is shorter than its diff:
```python
import functools

import jax
import jax.numpy as jnp
from jax import lax
from jax.experimental import pallas as pl
from jax.experimental.pallas import tpu as pltpu
from jax.sharding import PartitionSpec as P

F32 = jnp.float32
BF16 = jnp.bfloat16
MESH = pl.DeviceIdType.MESH


def dot(left, right):
    return jnp.dot(left, right, preferred_element_type=F32)


def dot_rows(left, right):
    return lax.dot_general(left, right, (((0,), (0,)), ((), ())), preferred_element_type=F32)


def kernel(
    n,
    listed,
    chains,
    pitches,
    owner_ref,
    pat_ref,
    low_index_ref,
    low_mask_ref,
    table_ref,
    source_ref,
    index_ref,
    mask_ref,
    par_ref,
    interp_ref,
    angle_ref,
    out_ref,
    phase_ref,
    op,
    couple,
    parent,
    arrived,
    wide,
    result,
    result_send,
    returned,
    own,
    given,
    buf,
    landed,
    far,
    own_wide,
    acc,
    out_send,
    out_recv,
    back_send,
    back_recv,
    swap_send,
    swap_recv,
    rs_send,
    rs_recv,
    ag_send,
    ag_recv,
):
    me = lax.axis_index("box")
    core = me % 2
    boxes = pat_ref.shape[1]
    kdir, illums = pat_ref.shape[2], pat_ref.shape[3]
    groups8 = boxes // 8
    qdir = interp_ref.shape[1]
    qloc = qdir // n
    both_own = 2 * boxes
    span = kdir // 2 // chains
    bits = list(range(1, n.bit_length() - 1))
    orders = [bits for _ in range(chains)]
    deep = len(bits) - 1
    kpitch, bpitch, qpitch, ppitch = pitches

    barrier = pltpu.get_barrier_semaphore()

    def greet(i, carry):
        peer = lax.rem(me + i, n)
        pl.semaphore_signal(barrier, inc=1, device_id={"box": peer}, device_id_type=MESH)
        return carry

    lax.fori_loop(1, n, greet, 0)

    unroll = 8
    for part in range(2):
        for b in range(boxes):
            spot = b // 8 * 16 + part * 8 + b % 8
            own_wide[pl.ds(spot * kpitch, kdir), :] = pat_ref[part, b].astype(F32)

    def turn(t, carry):
        for u in range(unroll):
            k = t * unroll + u
            own[k] = own_wide[pl.ds(k, both_own, stride=kpitch), :].astype(BF16)
        return carry

    lax.fori_loop(0, kdir // unroll, turn, 0)

    def remote(src, dst, send, recv, bit):
        mine = me // (1 << bit) % 2
        return pltpu.make_async_remote_copy(
            src_ref=src,
            dst_ref=dst,
            send_sem=send,
            recv_sem=recv,
            device_id={"box": me + (1 - 2 * mine) * (1 << bit)},
            device_id_type=MESH,
        )

    def swap(chain):
        spots = own.at[pl.ds((1 - core) * (kdir // 2) + chain * span, span)]
        return remote(spots, given[chain], swap_send.at[chain], swap_recv.at[chain], 0)

    def place(chain, depth):
        low = core * (kdir // 2) + chain * span
        size = span
        for b in orders[chain][:depth]:
            size = size // 2
            low = low + me // (1 << b) % 2 * size
        return low, size

    def reduction(chain, depth):
        bit = orders[chain][depth]
        low, size = place(chain, depth)
        if depth < deep:
            size = size // 2
            low = low + (1 - me // (1 << bit) % 2) * size
        spot = chain * span + span - (span >> depth)
        return remote(
            buf.at[pl.ds(low, size)],
            landed.at[pl.ds(spot, size)],
            rs_send.at[chain, depth],
            rs_recv.at[chain, depth],
            bit,
        )

    def reduce(chain, depth):
        reduction(chain, depth).wait()
        low, size = place(chain, min(depth + 1, deep))
        spot = chain * span + span - (span >> depth)
        target = far if depth == deep else buf
        target[pl.ds(low, size)] = buf[pl.ds(low, size)] + landed[pl.ds(spot, size)]
        if depth < deep:
            reduction(chain, depth + 1).start()
        else:
            doubling(chain, deep).start()

    def doubling(chain, depth):
        low, size = place(chain, depth)
        bit = orders[chain][depth - 1] if depth else 0
        spots = far.at[pl.ds(low, size)]
        return remote(spots, spots, ag_send.at[chain, depth], ag_recv.at[chain, depth], bit)

    def double(chain, depth):
        doubling(chain, depth).wait()
        doubling(chain, depth - 1).start()

    def merge(chain):
        swap(chain).wait()
        low, size = place(chain, 0)
        for step in range(listed):
            owner = owner_ref[step]
            device = owner // groups8
            rows = pl.ds(owner % groups8 * 16, 16)
            block = own[pl.ds(low, size), rows, :]
            theirs = given[chain][:, rows, :]
            block = jnp.where(device == me, block, jnp.where(device // 2 == me // 2, theirs, jnp.zeros_like(block)))
            buf[pl.ds(low, size), step * 16 : step * 16 + 16, :] = block
        reduction(chain, 0).start()

    phase_ref[:, :8] = jnp.cos(angle_ref[...]).T
    phase_ref[:, 8:] = jnp.sin(angle_ref[...]).T

    def out_copy(i, parent_at):
        peer = lax.rem(me + i, n)
        return pltpu.make_async_remote_copy(
            src_ref=parent.at[pl.ds(2 * parent_at, 2), pl.ds(pl.multiple_of(peer * qloc, qloc), qloc), :],
            dst_ref=arrived.at[me, pl.ds(2 * parent_at, 2)],
            send_sem=out_send.at[parent_at],
            recv_sem=out_recv.at[parent_at],
            device_id={"box": peer},
            device_id_type=MESH,
        )

    tile = 256
    def lift_parent(parent_at):
        def lift(t, carry):
            at = pl.multiple_of(t * tile, tile)
            left = interp_ref[:, pl.ds(at, tile)].T
            real = jnp.zeros((tile, illums), F32)
            imag = jnp.zeros((tile, illums), F32)
            for child in range(8):
                b = parent_at * 8 + child
                both = dot(left, jnp.concatenate([pat_ref[0, b], pat_ref[1, b]], axis=1))
                cosine = phase_ref[pl.ds(at, tile), child : child + 1]
                sine = phase_ref[pl.ds(at, tile), 8 + child : 9 + child]
                re, im = both[:, :illums], both[:, illums:]
                real = real + (cosine * re - sine * im)
                imag = imag + (cosine * im + sine * re)
            parent[2 * parent_at, pl.ds(at, tile), :] = real.astype(BF16)
            parent[2 * parent_at + 1, pl.ds(at, tile), :] = imag.astype(BF16)
            return carry

        lax.fori_loop(0, qdir // tile, lift, 0)

    def send_out(parent_at, low, high):
        def start_out(i, carry):
            out_copy(i, parent_at).start()
            return carry

        lax.fori_loop(low, high, start_out, 0)

    parents = n * groups8
    parents2 = 2 * parents

    def build_couple():
        lanes = lax.broadcasted_iota(jnp.int32, (parents, parents), 1)
        code = jnp.zeros((parents, parents), jnp.int32)
        slot_code = jnp.where(mask_ref[...] > 0, index_ref[...] + 1, 0).T
        slot_source = source_ref[...].T
        for j in range(source_ref.shape[0]):
            code = code + jnp.where(slot_source[:, j : j + 1] == lanes, slot_code[:, j : j + 1], 0)
        code = jnp.concatenate([code, code], axis=1) - 1
        each = max(1, 256 // parents2)
        kinds = lax.broadcasted_iota(jnp.int32, (par_ref.shape[1], each * parents2), 0)
        first = lax.broadcasted_iota(jnp.int32, (qloc, parents2), 1) < parents
        for p in range(0, parents, each):
            row = jnp.concatenate([code[p + u : p + u + 1] for u in range(each)], axis=1)
            hot = jnp.where(kinds == row, 1.0, 0.0).astype(BF16)
            got = [dot_rows(par_ref[part], hot) for part in range(2)]
            for u in range(each):
                real = got[0][:, u * parents2 : (u + 1) * parents2]
                imag = got[1][:, u * parents2 : (u + 1) * parents2]
                couple[pl.ds(p + u, qloc, stride=ppitch), :] = jnp.where(first, real, -imag)
                couple[pl.ds(parents + p + u, qloc, stride=ppitch), :] = jnp.where(first, imag, real)

    def build_op():
        sources = low_index_ref.shape[1]
        width = 2 * sources + -2 * sources % 128
        wanted = jnp.where(low_mask_ref[...] > 0, low_index_ref[...] + 1, 0)
        column = lax.broadcasted_iota(jnp.int32, (sources, width), 1)
        spread = lax.broadcasted_iota(jnp.int32, (sources, width), 0) == column // 16 * 8 + column % 8
        spread = jnp.where(spread, 1.0, 0.0).astype(BF16)
        high = dot((wanted // 16).astype(F32).astype(BF16), spread)
        rest = dot((wanted % 16).astype(F32).astype(BF16), spread)
        code = (16 * high + rest).astype(jnp.int32) - 1
        low_kinds = lax.broadcasted_iota(jnp.int32, (table_ref.shape[1], 2 * width), 0)
        low_first = lax.broadcasted_iota(jnp.int32, (kdir, width), 1) // 8 % 2 == 0
        for b in range(0, boxes, 2):
            row = jnp.concatenate([code[b : b + 1], code[b + 1 : b + 2]], axis=1)
            hot = jnp.where(low_kinds == row, 1.0, 0.0).astype(BF16)
            got = [dot_rows(table_ref[part], hot) for part in range(2)]
            for u in range(2):
                real = got[0][:, u * width : (u + 1) * width]
                imag = got[1][:, u * width : (u + 1) * width]
                op[pl.ds(b + u, kdir, stride=bpitch), :] = jnp.where(low_first, real, -imag)
                op[pl.ds(boxes + b + u, kdir, stride=bpitch), :] = jnp.where(low_first, imag, real)

    def widen(source, value):
        for part in range(2):
            for p in range(groups8):
                s = (part * n + source) * groups8 + p
                at = pl.multiple_of(s * qpitch, 8)
                wide[pl.ds(at, qloc), :] = value(p * 2 + part).astype(F32)

    def back_copy(i):
        peer = lax.rem(me + i, n)
        return pltpu.make_async_remote_copy(
            src_ref=result_send.at[:, pl.ds(peer * groups8, groups8)],
            dst_ref=returned.at[:, :, pl.ds(pl.multiple_of(me * qloc, qloc), qloc), :],
            send_sem=back_send.at[0],
            recv_sem=back_recv.at[0],
            device_id={"box": peer},
            device_id_type=MESH,
        )

    def exchange():
        widen(me, lambda c: parent[c, pl.ds(pl.multiple_of(me * qloc, qloc), qloc), :])

        for parent_at in range(groups8):
            whole = arrived.at[pl.ds(0, n - 1), pl.ds(2 * parent_at, 2)]
            remote(whole, whole, out_send.at[parent_at], out_recv.at[parent_at], 0).wait()

        def take(i, carry):
            source = lax.rem(me - i + n, n)
            widen(source, lambda c: arrived[source, c])
            return carry

        lax.fori_loop(1, n, take, 0)

        def translate(t, carry):
            for u in range(unroll):
                q = t * unroll + u
                sources = wide[pl.ds(q, parents2, stride=qpitch), :].astype(BF16)
                result[pl.ds(q, parents2, stride=qpitch), :] = dot(
                    couple[pl.ds(pl.multiple_of(q * ppitch, 8), parents2), :].astype(BF16), sources
                )
            return carry

        lax.fori_loop(0, qloc // unroll, translate, 0)
        for s in range(parents2):
            result_send[s // parents, s % parents] = result[pl.ds(s * qpitch, qloc), :].astype(BF16)

    def send_back():
        def start_back(i, carry):
            back_copy(i).start()
            return carry

        lax.fori_loop(1, n, start_back, 0)
        returned[:, :, pl.ds(pl.multiple_of(me * qloc, qloc), qloc), :] = result_send[:, pl.ds(me * groups8, groups8)]

    def near(at):
        def one(t, carry):
            sums = []
            for u in range(unroll):
                k = at + t * unroll + u
                operator = op[pl.ds(pl.multiple_of(k * bpitch, 8), both_own), :].astype(BF16)
                sources = jnp.concatenate([own[k], far[k]], axis=0)
                sums.append(dot(operator[:, : both_own + 16 * listed], sources))
            for u in range(unroll):
                acc[pl.ds(at + t * unroll + u, both_own, stride=kpitch), :] = sums[u]
            return carry

        lax.fori_loop(0, span // unroll, one, 0)

    def finish():
        whole = returned.at[:, :, pl.ds(0, (n - 1) * qloc), :]
        remote(whole, whole, back_send.at[0], back_recv.at[0], 0).wait()
        for parent_at in range(groups8):
            for child in range(8):
                b = parent_at * 8 + child
                re = returned[0, parent_at].astype(F32)
                im = returned[1, parent_at].astype(F32)
                cosine = phase_ref[:, child : child + 1]
                sine = phase_ref[:, 8 + child : 9 + child]
                real = (cosine * re + sine * im).astype(BF16)
                imag = (cosine * im - sine * re).astype(BF16)
                both = dot(interp_ref[...], jnp.concatenate([real, imag], axis=1))
                out_ref[pl.ds(b * kdir, kdir), :] = both[:, :illums] + acc[pl.ds(b * kpitch, kdir), :]
                out_ref[pl.ds((boxes + b) * kdir, kdir), :] = (
                    both[:, illums:] + acc[pl.ds((boxes + b) * kpitch, kdir), :]
                )

    last_step = 2 * deep + 1

    def far_step(chain, step):
        if step <= deep:
            reduce(chain, step)
        elif step < last_step:
            double(chain, last_step - step)
            if step == last_step - 1:
                near(core * (kdir // 2) + chain * span)
        else:
            doubling(chain, 0).wait()
            near((1 - core) * (kdir // 2) + chain * span)

    def far_slot(slot):
        for chain in range(chains):
            if 0 <= slot - chain <= last_step:
                far_step(chain, slot - chain)

    slots = chains + last_step

    lift_parent(0)
    lift_parent(1)
    build_couple()
    build_op()
    pl.semaphore_wait(barrier, n - 1)
    for chain in range(chains):
        swap(chain).start()

    send_out(0, 1, n)
    for chain in range(chains):
        merge(chain)
    send_out(1, 1, n)
    for slot in range(5): far_slot(slot)
    exchange()
    send_back()
    for slot in range(5, slots): far_slot(slot)
    finish()


def shards(
    patterns,
    owner_block,
    low_index,
    low_mask,
    low_table,
    interp,
    shift_angle,
    par_source,
    par_index,
    par_mask,
    par_table,
):
    boxes, kdir, illums = patterns.shape[1:]
    groups8 = boxes // 8
    qdir = interp.shape[1]
    n = lax.axis_size("box")
    listed = owner_block.shape[0]
    parents = par_source.shape[0]
    qloc = qdir // n
    sources = low_index.shape[1]
    chains = 4

    start = lax.axis_index("box") * qloc
    table = lax.dynamic_slice_in_dim(par_table, start, qloc, 2)

    pitches = (kdir + 8, 2 * boxes + 8, qloc + 8, 2 * parents + 8)
    kpitch, bpitch, qpitch, ppitch = pitches
    vmem = pl.BlockSpec(memory_space=pltpu.VMEM)
    smem = pl.BlockSpec(memory_space=pltpu.SMEM)
    stages = n.bit_length() - 1
    dma = pltpu.SemaphoreType.DMA
    return pl.pallas_call(
        functools.partial(kernel, n, listed, chains, pitches),
        out_shape=jax.ShapeDtypeStruct((2 * boxes * kdir, illums), F32),
        in_specs=[smem] + [vmem] * 10,
        out_specs=vmem,
        scratch_shapes=[
            pltpu.VMEM((qdir, 16), F32),
            pltpu.VMEM((kdir * bpitch, 2 * sources + -2 * sources % 128), F32),
            pltpu.VMEM((qloc * ppitch, 2 * parents), F32),
            pltpu.VMEM((2 * groups8, qdir, illums), BF16),
            pltpu.VMEM((n, 2 * groups8, qloc, illums), BF16),
            pltpu.VMEM((2 * parents * qpitch, illums), F32),
            pltpu.VMEM((2 * parents * qpitch, illums), F32),
            pltpu.VMEM((2, parents, qloc, illums), BF16),
            pltpu.VMEM((2, groups8, qdir, illums), BF16),
            pltpu.VMEM((kdir, 2 * boxes, illums), BF16),
            [pltpu.VMEM((kdir // 2 // chains, 2 * boxes, illums), BF16) for _ in range(chains)],
            pltpu.VMEM((kdir, 16 * listed, illums), BF16),
            pltpu.VMEM((kdir // 2, 16 * listed, illums), BF16),
            pltpu.VMEM((kdir, 16 * listed, illums), BF16),
            pltpu.VMEM((2 * boxes * kpitch, illums), F32),
            pltpu.VMEM((2 * boxes * kpitch, illums), F32),
            dma((groups8,)),
            dma((groups8,)),
            dma((1,)),
            dma((1,)),
            dma((chains,)),
            dma((chains,)),
            dma((chains, stages - 1)),
            dma((chains, stages - 1)),
            dma((chains, stages - 1)),
            dma((chains, stages - 1)),
        ],
        compiler_params=pltpu.CompilerParams(
            collective_id=0, has_side_effects=True, vmem_limit_bytes=56 * 1024 * 1024
        ),
    )(
        owner_block,
        patterns,
        low_index,
        low_mask,
        low_table,
        par_source.T,
        par_index.T,
        par_mask.T,
        table,
        interp,
        shift_angle,
    ).reshape(2, boxes, kdir, illums)


def solution(mesh):
    placed = (
        P(None, "box", None, "illum"),
        P(),
        P("box", None),
        P("box", None),
        P(),
        P(),
        P(),
        P(),
        P(),
        P(),
        P(),
    )
    return jax.shard_map(
        shards, mesh=mesh, in_specs=placed, out_specs=P(None, "box", None, "illum"), check_vma=False
    )
```

time: 73.2 us -> 68.7 us (0.939)
  Pallas kernels: 64.7 us -> 61.7 us
  local copies, waits for them, and re-layouts: 8.17 us -> 6.77 us
    pallas_call x1, Pallas kernels: 64.7 us -> 61.7 us  [shards(): pl.pallas_call(functools.partial(kernel, n, listed, chains, pitches), out...]
    transpose x3 -> x0, local copies, waits for them, and re-layouts: 2.74 us -> none  [the longest x1 1.74 us: shards(): low = jnp.transpose(low_table, (0, 2, 1)).reshape(2 * kdir, -1)]
    unnamed x5, local copies, waits for them, and re-layouts: 4.76 us -> 6.53 us
where the time goes in v2:
time: 68.7 us; the launch traced here: 68.5 us
  Pallas kernels  61.7 us (90%)
  local copies, waits for them, and re-layouts  6.77 us (10%)
    pallas_call x1, Pallas kernels, shards(): pl.pallas_call(functools.partial(kernel, n, listed, chains, pitches), out...  61.7 us
    unnamed x5, local copies, waits for them, and re-layouts  6.53 us

profile of v2, /device:TPU:0, one launch (start us, length us, event | category | flops | bytes accessed | tf_op | source)
XLA Modules:
  0.0 68.5 jit_solution(1928358296146400800)
XLA Ops:
  0.0 0.0 copy-start
  0.0 1.1 %copy-done = bf16[2,316,512]{2,0,1:T(2,128)(2,1)S(1)} copy-done((bf16[2,316,512]{2,0,1:T(2,128)(2,1)S(1)}, bf16[2,316,512]{2,0,1:T(2,128)(2,1)}, u32[]{:S(2)}) %copy-start) | copy-done | bytes 647192
  1.1 0.2 constant_dynamic-slice_fusion
  1.3 0.7 %copy.14.par_ref = bf16[2,316,32]{2,1,0:T(8,128)(2,1)} copy(bf16[2,316,32]{2,0,1:T(2,128)(2,1)S(1)} %constant_dynamic-slice_fusion) | data formatting | bytes 80896
  2.0 1.6 %copy.13.table_ref = bf16[2,316,128]{2,1,0:T(8,128)(2,1)} copy(bf16[2,316,128]{2,0,1:T(2,128)(2,1)} %param.15) | data formatting | bytes 323584 | tf_op args[4]
  3.6 61.7 %shard_map.109 = f32[4096,128]{1,0:T(8,128)} custom-call(s32[4]{0:T(128)} %owner_ref.1, bf16[2,16,128,128]{3,2,1,0:T(8,128)(2,1)} %pat_ref.1, s32[16,48]{1,0:T(8,128)} %low_index_ref.1, s32[16,48]{1,0:T(8,128)} %low_mask_ref.1, bf16[2,316,128]{2,1,0:T(8,128)(2,1)} %copy.13.table_ref, s32[16,32]{1,0:T(8,128)} %bitcast.5, s32[16,32]{1,0:T(8,128)} %bitcast.6, ...), custom_call_target="tpu_custom_call" | custom-call | tf_op jit(solution)/shard_map/pallas_call | solution.py:420
  65.3 3.1 %copy.16 = f32[2,16,128,128]{3,2,1,0:T(8,128)} copy(f32[2,16,128,128]{3,2,1,0:T(8,128)} %bitcast.4) | data formatting | bytes 4194304
Async XLA Ops:
  0.0 1.1 %copy-start = (bf16[2,316,512]{2,0,1:T(2,128)(2,1)S(1)}, bf16[2,316,512]{2,0,1:T(2,128)(2,1)}, u32[]{:S(2)}) copy-start(bf16[2,316,512]{2,0,1:T(2,128)(2,1)} %param.21) | copy-start | bytes 1941508

commit v3 on v2

--- a/solution.py
+++ b/solution.py
@@ -268,13 +268,13 @@
                 at = pl.multiple_of(s * qpitch, 8)
                 wide[pl.ds(at, qloc), :] = value(p * 2 + part).astype(F32)
 
-    def back_copy(i):
+    def back_copy(i, parent_at):
         peer = lax.rem(me + i, n)
         return pltpu.make_async_remote_copy(
-            src_ref=result_send.at[:, pl.ds(peer * groups8, groups8)],
-            dst_ref=returned.at[:, :, pl.ds(pl.multiple_of(me * qloc, qloc), qloc), :],
-            send_sem=back_send.at[0],
-            recv_sem=back_recv.at[0],
+            src_ref=result_send.at[:, pl.ds(peer * groups8 + parent_at, 1)],
+            dst_ref=returned.at[parent_at, :, :, pl.ds(pl.multiple_of(me * qloc, qloc), qloc), :],
+            send_sem=back_send.at[parent_at],
+            recv_sem=back_recv.at[parent_at],
             device_id={"box": peer},
             device_id_type=MESH,
         )
@@ -306,13 +306,17 @@
         for s in range(parents2):
             result_send[s // parents, s % parents] = result[pl.ds(s * qpitch, qloc), :].astype(BF16)
 
-    def send_back():
+    def send_back(parent_at, low, high):
         def start_back(i, carry):
-            back_copy(i).start()
-            return carry
-
-        lax.fori_loop(1, n, start_back, 0)
-        returned[:, :, pl.ds(pl.multiple_of(me * qloc, qloc), qloc), :] = result_send[:, pl.ds(me * groups8, groups8)]
+            back_copy(i, parent_at).start()
+            return carry
+
+        lax.fori_loop(low, high, start_back, 0)
+
+    def keep_back():
+        mine = pl.ds(pl.multiple_of(me * qloc, qloc), qloc)
+        for parent_at in range(groups8):
+            returned[parent_at, :, :, mine, :] = result_send[:, pl.ds(me * groups8 + parent_at, 1)]
 
     def near(at):
         def one(t, carry):
@@ -328,23 +332,25 @@
 
         lax.fori_loop(0, span // unroll, one, 0)
 
-    def finish():
-        whole = returned.at[:, :, pl.ds(0, (n - 1) * qloc), :]
-        remote(whole, whole, back_send.at[0], back_recv.at[0], 0).wait()
-        for parent_at in range(groups8):
-            for child in range(8):
-                b = parent_at * 8 + child
-                re = returned[0, parent_at].astype(F32)
-                im = returned[1, parent_at].astype(F32)
-                cosine = phase_ref[:, child : child + 1]
-                sine = phase_ref[:, 8 + child : 9 + child]
-                real = (cosine * re + sine * im).astype(BF16)
-                imag = (cosine * im - sine * re).astype(BF16)
-                both = dot(interp_ref[...], jnp.concatenate([real, imag], axis=1))
-                out_ref[pl.ds(b * kdir, kdir), :] = both[:, :illums] + acc[pl.ds(b * kpitch, kdir), :]
-                out_ref[pl.ds((boxes + b) * kdir, kdir), :] = (
-                    both[:, illums:] + acc[pl.ds((boxes + b) * kpitch, kdir), :]
-                )
+    def down(parent_at):
+        whole = returned.at[parent_at, :, :, pl.ds(0, (n - 1) * qloc), :]
+        remote(whole, whole, back_send.at[parent_at], back_recv.at[parent_at], 0).wait()
+        for child in range(8):
+            b = parent_at * 8 + child
+            re = returned[parent_at, 0, 0].astype(F32)
+            im = returned[parent_at, 1, 0].astype(F32)
+            cosine = phase_ref[:, child : child + 1]
+            sine = phase_ref[:, 8 + child : 9 + child]
+            real = (cosine * re + sine * im).astype(BF16)
+            imag = (cosine * im - sine * re).astype(BF16)
+            both = dot(interp_ref[...], jnp.concatenate([real, imag], axis=1))
+            out_ref[pl.ds(b * kdir, kdir), :] = both[:, :illums]
+            out_ref[pl.ds((boxes + b) * kdir, kdir), :] = both[:, illums:]
+
+    def settle():
+        for b in range(both_own):
+            spots = pl.ds(b * kdir, kdir)
+            out_ref[spots, :] = out_ref[spots, :] + acc[pl.ds(b * kpitch, kdir), :]
 
     last_step = 2 * deep + 1
 
@@ -360,30 +366,36 @@
             near((1 - core) * (kdir // 2) + chain * span)
 
     def far_slot(slot):
-        for chain in range(chains):
+        for chain in reversed(range(chains)):
             if 0 <= slot - chain <= last_step:
                 far_step(chain, slot - chain)
 
     slots = chains + last_step
-
     lift_parent(0)
     lift_parent(1)
     build_couple()
     build_op()
     pl.semaphore_wait(barrier, n - 1)
-    for chain in range(chains):
-        swap(chain).start()
-
+    for chain in range(chains): swap(chain).start()
     send_out(0, 1, n)
-    for chain in range(chains):
-        merge(chain)
+    for chain in range(chains): merge(chain)
     send_out(1, 1, n)
-    for slot in range(5): far_slot(slot)
+    far_slot(0)
+    far_slot(1)
+    far_slot(2)
+    far_slot(3)
+    far_slot(4)
     exchange()
-    send_back()
-    for slot in range(5, slots): far_slot(slot)
-    finish()
-
+    send_back(0, 1, n)
+    send_back(1, 1, n)
+    keep_back()
+    far_slot(5)
+    far_slot(6)
+    down(0)
+    far_slot(7)
+    down(1)
+    far_slot(8)
+    settle()
 
 def shards(
     patterns,
@@ -431,7 +443,7 @@
             pltpu.VMEM((2 * parents * qpitch, illums), F32),
             pltpu.VMEM((2 * parents * qpitch, illums), F32),
             pltpu.VMEM((2, parents, qloc, illums), BF16),
-            pltpu.VMEM((2, groups8, qdir, illums), BF16),
+            pltpu.VMEM((groups8, 2, 1, qdir, illums), BF16),
             pltpu.VMEM((kdir, 2 * boxes, illums), BF16),
             [pltpu.VMEM((kdir // 2 // chains, 2 * boxes, illums), BF16) for _ in range(chains)],
             pltpu.VMEM((kdir, 16 * listed, illums), BF16),
@@ -441,8 +453,8 @@
             pltpu.VMEM((2 * boxes * kpitch, illums), F32),
             dma((groups8,)),
             dma((groups8,)),
-            dma((1,)),
-            dma((1,)),
+            dma((groups8,)),
+            dma((groups8,)),
             dma((chains,)),
             dma((chains,)),
             dma((chains, stages - 1)),

time: 68.7 us -> 63.8 us (0.929)
  Pallas kernels: 61.7 us -> 56.7 us
    pallas_call x1, Pallas kernels: 61.7 us -> 56.7 us  [shards(): pl.pallas_call(functools.partial(kernel, n, listed, chains, pitches), out...]
where the time goes in v3:
time: 63.8 us; the launch traced here: 63.5 us
  Pallas kernels  56.7 us (89%)
  local copies, waits for them, and re-layouts  6.77 us (11%)
    pallas_call x1, Pallas kernels, shards(): pl.pallas_call(functools.partial(kernel, n, listed, chains, pitches), out...  56.7 us
    unnamed x5, local copies, waits for them, and re-layouts  6.53 us

profile of v3, /device:TPU:0, one launch (start us, length us, event | category | flops | bytes accessed | tf_op | source)
XLA Modules:
  0.0 63.5 jit_solution(15131410884865694388)
XLA Ops:
  0.0 0.0 copy-start
  0.0 1.1 %copy-done = bf16[2,316,512]{2,0,1:T(2,128)(2,1)S(1)} copy-done((bf16[2,316,512]{2,0,1:T(2,128)(2,1)S(1)}, bf16[2,316,512]{2,0,1:T(2,128)(2,1)}, u32[]{:S(2)}) %copy-start) | copy-done | bytes 647192
  1.1 0.2 constant_dynamic-slice_fusion
  1.3 0.7 %copy.14.par_ref = bf16[2,316,32]{2,1,0:T(8,128)(2,1)} copy(bf16[2,316,32]{2,0,1:T(2,128)(2,1)S(1)} %constant_dynamic-slice_fusion) | data formatting | bytes 80896
  2.0 1.6 %copy.13.table_ref = bf16[2,316,128]{2,1,0:T(8,128)(2,1)} copy(bf16[2,316,128]{2,0,1:T(2,128)(2,1)} %param.15) | data formatting | bytes 323584 | tf_op args[4]
  3.6 56.7 %shard_map.109 = f32[4096,128]{1,0:T(8,128)} custom-call(s32[4]{0:T(128)} %owner_ref.1, bf16[2,16,128,128]{3,2,1,0:T(8,128)(2,1)} %pat_ref.1, s32[16,48]{1,0:T(8,128)} %low_index_ref.1, s32[16,48]{1,0:T(8,128)} %low_mask_ref.1, bf16[2,316,128]{2,1,0:T(8,128)(2,1)} %copy.13.table_ref, s32[16,32]{1,0:T(8,128)} %bitcast.5, s32[16,32]{1,0:T(8,128)} %bitcast.6, ...), custom_call_target="tpu_custom_call" | custom-call | tf_op jit(solution)/shard_map/pallas_call | solution.py:432
  60.4 3.1 %copy.16 = f32[2,16,128,128]{3,2,1,0:T(8,128)} copy(f32[2,16,128,128]{3,2,1,0:T(8,128)} %bitcast.4) | data formatting | bytes 4194304
Async XLA Ops:
  0.0 1.1 %copy-start = (bf16[2,316,512]{2,0,1:T(2,128)(2,1)S(1)}, bf16[2,316,512]{2,0,1:T(2,128)(2,1)}, u32[]{:S(2)}) copy-start(bf16[2,316,512]{2,0,1:T(2,128)(2,1)} %param.21) | copy-start | bytes 1941508

commit v4 on v3

--- a/solution.py
+++ b/solution.py
@@ -176,8 +176,17 @@
     phase_ref[:, :8] = jnp.cos(angle_ref[...]).T
     phase_ref[:, 8:] = jnp.sin(angle_ref[...]).T
 
+    def peer_of(i):
+        peer = me
+        for b in range(n.bit_length() - 1):
+            if i >> b & 1:
+                peer = peer + (1 - 2 * (me // (1 << b) % 2)) * (1 << b)
+        return peer
+
+    tour = list(range(n - 1, 0, -1))
+
     def out_copy(i, parent_at):
-        peer = lax.rem(me + i, n)
+        peer = peer_of(i)
         return pltpu.make_async_remote_copy(
             src_ref=parent.at[pl.ds(2 * parent_at, 2), pl.ds(pl.multiple_of(peer * qloc, qloc), qloc), :],
             dst_ref=arrived.at[me, pl.ds(2 * parent_at, 2)],
@@ -208,12 +217,9 @@
 
         lax.fori_loop(0, qdir // tile, lift, 0)
 
-    def send_out(parent_at, low, high):
-        def start_out(i, carry):
+    def send_out(parent_at):
+        for i in tour:
             out_copy(i, parent_at).start()
-            return carry
-
-        lax.fori_loop(low, high, start_out, 0)
 
     parents = n * groups8
     parents2 = 2 * parents
@@ -269,7 +275,7 @@
                 wide[pl.ds(at, qloc), :] = value(p * 2 + part).astype(F32)
 
     def back_copy(i, parent_at):
-        peer = lax.rem(me + i, n)
+        peer = peer_of(i)
         return pltpu.make_async_remote_copy(
             src_ref=result_send.at[:, pl.ds(peer * groups8 + parent_at, 1)],
             dst_ref=returned.at[parent_at, :, :, pl.ds(pl.multiple_of(me * qloc, qloc), qloc), :],
@@ -306,12 +312,9 @@
         for s in range(parents2):
             result_send[s // parents, s % parents] = result[pl.ds(s * qpitch, qloc), :].astype(BF16)
 
-    def send_back(parent_at, low, high):
-        def start_back(i, carry):
+    def send_back(parent_at):
+        for i in tour:
             back_copy(i, parent_at).start()
-            return carry
-
-        lax.fori_loop(low, high, start_back, 0)
 
     def keep_back():
         mine = pl.ds(pl.multiple_of(me * qloc, qloc), qloc)
@@ -359,43 +362,47 @@
             reduce(chain, step)
         elif step < last_step:
             double(chain, last_step - step)
-            if step == last_step - 1:
-                near(core * (kdir // 2) + chain * span)
         else:
             doubling(chain, 0).wait()
-            near((1 - core) * (kdir // 2) + chain * span)
 
     def far_slot(slot):
-        for chain in reversed(range(chains)):
-            if 0 <= slot - chain <= last_step:
-                far_step(chain, slot - chain)
+        live = [chain for chain in reversed(range(chains)) if 0 <= slot - chain <= last_step]
+        for chain in live:
+            far_step(chain, slot - chain)
+        for chain in live:
+            if slot - chain == last_step - 1:
+                near(core * (kdir // 2) + chain * span)
+            if slot - chain == last_step:
+                near((1 - core) * (kdir // 2) + chain * span)
 
     slots = chains + last_step
-    lift_parent(0)
-    lift_parent(1)
+    for parent_at in range(groups8):
+        lift_parent(parent_at)
     build_couple()
     build_op()
     pl.semaphore_wait(barrier, n - 1)
-    for chain in range(chains): swap(chain).start()
-    send_out(0, 1, n)
-    for chain in range(chains): merge(chain)
-    send_out(1, 1, n)
-    far_slot(0)
-    far_slot(1)
-    far_slot(2)
-    far_slot(3)
-    far_slot(4)
+    for chain in range(chains):
+        swap(chain).start()
+    send_out(0)
+    for chain in range(chains):
+        merge(chain)
+    for parent_at in range(1, groups8):
+        send_out(parent_at)
+    for slot in range(slots - 4):
+        far_slot(slot)
     exchange()
-    send_back(0, 1, n)
-    send_back(1, 1, n)
+    for parent_at in range(groups8):
+        send_back(parent_at)
     keep_back()
-    far_slot(5)
-    far_slot(6)
+    far_slot(slots - 4)
+    far_slot(slots - 3)
     down(0)
-    far_slot(7)
-    down(1)
-    far_slot(8)
+    far_slot(slots - 2)
+    for parent_at in range(1, groups8):
+        down(parent_at)
+    far_slot(slots - 1)
     settle()
+
 
 def shards(
     patterns,

time: 63.8 us -> 63.3 us (level)
  no operation moved by 1% of the time
where the time goes in v4:
time: 63.3 us; the launch traced here: 63 us
  Pallas kernels  56.3 us (89%)
  local copies, waits for them, and re-layouts  6.77 us (11%)
    pallas_call x1, Pallas kernels, shards(): pl.pallas_call(functools.partial(kernel, n, listed, chains, pitches), out...  56.3 us
    unnamed x5, local copies, waits for them, and re-layouts  6.53 us

profile of v4, /device:TPU:0, one launch (start us, length us, event | category | flops | bytes accessed | tf_op | source)
XLA Modules:
  0.0 63.0 jit_solution(15522925358792231753)
XLA Ops:
  0.0 0.0 copy-start
  0.0 1.1 %copy-done = bf16[2,316,512]{2,0,1:T(2,128)(2,1)S(1)} copy-done((bf16[2,316,512]{2,0,1:T(2,128)(2,1)S(1)}, bf16[2,316,512]{2,0,1:T(2,128)(2,1)}, u32[]{:S(2)}) %copy-start) | copy-done | bytes 647192
  1.1 0.2 constant_dynamic-slice_fusion
  1.3 0.7 %copy.14.par_ref = bf16[2,316,32]{2,1,0:T(8,128)(2,1)} copy(bf16[2,316,32]{2,0,1:T(2,128)(2,1)S(1)} %constant_dynamic-slice_fusion) | data formatting | bytes 80896
  2.0 1.6 %copy.13.table_ref = bf16[2,316,128]{2,1,0:T(8,128)(2,1)} copy(bf16[2,316,128]{2,0,1:T(2,128)(2,1)} %param.15) | data formatting | bytes 323584 | tf_op args[4]
  3.6 56.3 %shard_map.109 = f32[4096,128]{1,0:T(8,128)} custom-call(s32[4]{0:T(128)} %owner_ref.1, bf16[2,16,128,128]{3,2,1,0:T(8,128)(2,1)} %pat_ref.1, s32[16,48]{1,0:T(8,128)} %low_index_ref.1, s32[16,48]{1,0:T(8,128)} %low_mask_ref.1, bf16[2,316,128]{2,1,0:T(8,128)(2,1)} %copy.13.table_ref, s32[16,32]{1,0:T(8,128)} %bitcast.5, s32[16,32]{1,0:T(8,128)} %bitcast.6, ...), custom_call_target="tpu_custom_call" | custom-call | tf_op jit(solution)/shard_map/pallas_call | solution.py:439
  59.9 3.1 %copy.16 = f32[2,16,128,128]{3,2,1,0:T(8,128)} copy(f32[2,16,128,128]{3,2,1,0:T(8,128)} %bitcast.4) | data formatting | bytes 4194304
Async XLA Ops:
  0.0 1.1 %copy-start = (bf16[2,316,512]{2,0,1:T(2,128)(2,1)S(1)}, bf16[2,316,512]{2,0,1:T(2,128)(2,1)}, u32[]{:S(2)}) copy-start(bf16[2,316,512]{2,0,1:T(2,128)(2,1)} %param.21) | copy-start | bytes 1941508

commit v5 on v4

--- a/solution.py
+++ b/solution.py
@@ -37,6 +37,8 @@
     interp_ref,
     angle_ref,
     out_ref,
+    low_wide,
+    par_wide,
     phase_ref,
     op,
     couple,
@@ -233,12 +235,20 @@
             code = code + jnp.where(slot_source[:, j : j + 1] == lanes, slot_code[:, j : j + 1], 0)
         code = jnp.concatenate([code, code], axis=1) - 1
         each = max(1, 256 // parents2)
-        kinds = lax.broadcasted_iota(jnp.int32, (par_ref.shape[1], each * parents2), 0)
+        par_wide[...] = par_ref[...].astype(F32)
+        lines = qdir // 128 * 2
+        entries = par_ref.shape[0] // lines
+        start = me * qloc
+        tables = []
+        for part in range(2):
+            wanted = par_wide[pl.ds(start // 128 * 2 + part, entries, stride=lines), :]
+            tables.append(pltpu.roll(wanted, (128 - start % 128) % 128, 1)[:, :qloc].astype(BF16))
+        kinds = lax.broadcasted_iota(jnp.int32, (entries, each * parents2), 0)
         first = lax.broadcasted_iota(jnp.int32, (qloc, parents2), 1) < parents
         for p in range(0, parents, each):
             row = jnp.concatenate([code[p + u : p + u + 1] for u in range(each)], axis=1)
             hot = jnp.where(kinds == row, 1.0, 0.0).astype(BF16)
-            got = [dot_rows(par_ref[part], hot) for part in range(2)]
+            got = [dot_rows(tables[part], hot) for part in range(2)]
             for u in range(each):
                 real = got[0][:, u * parents2 : (u + 1) * parents2]
                 imag = got[1][:, u * parents2 : (u + 1) * parents2]
@@ -255,12 +265,15 @@
         high = dot((wanted // 16).astype(F32).astype(BF16), spread)
         rest = dot((wanted % 16).astype(F32).astype(BF16), spread)
         code = (16 * high + rest).astype(jnp.int32) - 1
-        low_kinds = lax.broadcasted_iota(jnp.int32, (table_ref.shape[1], 2 * width), 0)
+        low_wide[...] = table_ref[...].astype(F32)
+        entries = table_ref.shape[0] // 2
+        tables = [low_wide[pl.ds(part, entries, stride=2), :].astype(BF16) for part in range(2)]
+        low_kinds = lax.broadcasted_iota(jnp.int32, (entries, 2 * width), 0)
         low_first = lax.broadcasted_iota(jnp.int32, (kdir, width), 1) // 8 % 2 == 0
         for b in range(0, boxes, 2):
             row = jnp.concatenate([code[b : b + 1], code[b + 1 : b + 2]], axis=1)
             hot = jnp.where(low_kinds == row, 1.0, 0.0).astype(BF16)
-            got = [dot_rows(table_ref[part], hot) for part in range(2)]
+            got = [dot_rows(tables[part], hot) for part in range(2)]
             for u in range(2):
                 real = got[0][:, u * width : (u + 1) * width]
                 imag = got[1][:, u * width : (u + 1) * width]
@@ -427,8 +440,8 @@
     sources = low_index.shape[1]
     chains = 4
 
-    start = lax.axis_index("box") * qloc
-    table = lax.dynamic_slice_in_dim(par_table, start, qloc, 2)
+    low_rows = jnp.transpose(low_table.reshape(2, -1, kdir // 128, 128), (1, 2, 0, 3)).reshape(-1, 128)
+    par_rows = jnp.transpose(par_table.reshape(2, -1, qdir // 128, 128), (1, 2, 0, 3)).reshape(-1, 128)
 
     pitches = (kdir + 8, 2 * boxes + 8, qloc + 8, 2 * parents + 8)
     kpitch, bpitch, qpitch, ppitch = pitches
@@ -442,6 +455,8 @@
         in_specs=[smem] + [vmem] * 10,
         out_specs=vmem,
         scratch_shapes=[
+            pltpu.VMEM(low_rows.shape, F32),
+            pltpu.VMEM(par_rows.shape, F32),
             pltpu.VMEM((qdir, 16), F32),
             pltpu.VMEM((kdir * bpitch, 2 * sources + -2 * sources % 128), F32),
             pltpu.VMEM((qloc * ppitch, 2 * parents), F32),
@@ -477,11 +492,11 @@
         patterns,
         low_index,
         low_mask,
-        low_table,
+        low_rows,
         par_source.T,
         par_index.T,
         par_mask.T,
-        table,
+        par_rows,
         interp,
         shift_angle,
     ).reshape(2, boxes, kdir, illums)

time: 63.3 us -> 59.7 us (0.943)
  local copies, waits for them, and re-layouts: 6.77 us -> 3.14 us
    unnamed x5 -> x1, local copies, waits for them, and re-layouts: 6.53 us -> 3.14 us
where the time goes in v5:
time: 59.7 us; the launch traced here: 59.5 us
  Pallas kernels  56.3 us (94%)
  local copies, waits for them, and re-layouts  3.14 us (5%)
    pallas_call x1, Pallas kernels, shards(): pl.pallas_call(functools.partial(kernel, n, listed, chains, pitches), out...  56.3 us
    unnamed x1, local copies, waits for them, and re-layouts  3.14 us

profile of v5, /device:TPU:0, one launch (start us, length us, event | category | flops | bytes accessed | tf_op | source)
XLA Modules:
  0.0 59.5 jit_solution(15700846407940950397)
XLA Ops:
  0.0 56.3 %shard_map.109 = f32[4096,128]{1,0:T(8,128)} custom-call(s32[4]{0:T(128)} %owner_ref.1, bf16[2,16,128,128]{3,2,1,0:T(8,128)(2,1)} %pat_ref.1, s32[16,48]{1,0:T(8,128)} %low_index_ref.1, s32[16,48]{1,0:T(8,128)} %low_mask_ref.1, bf16[632,128]{1,0:T(8,128)(2,1)} %bitcast.16, s32[16,32]{1,0:T(8,128)} %bitcast.17, s32[16,32]{1,0:T(8,128)} %bitcast.18, ...), custom_call_target="tpu_custom_call" | custom-call | tf_op jit(solution)/shard_map/pallas_call | solution.py:452
  56.3 3.1 %copy.14 = f32[2,16,128,128]{3,2,1,0:T(8,128)} copy(f32[2,16,128,128]{3,2,1,0:T(8,128)} %bitcast.14) | data formatting | bytes 4194304
